TPU v7x, 32 devices: a whole 2x2x4 slice. The times are simulated.
32 devices in a mesh: zrow: 4 (over z), zcol: 8 (over y, x, core).
Axes of the slice: x: 2, y: 2, z: 4, core: 2. Of those that a mesh axis runs over, the one named last changes fastest.
Arguments:
- state: float32 [64, 8, 32768], P(None, None, ('zrow', 'zcol')), may hold values from -6 to 6
- kernel: float32 [32768], P(('zrow', 'zcol')), may hold values from 0.5 to 5
- blocks: int32 [2048, 4], replicated, may hold values from 0 to 255
- foot_weight: float32 [2048, 4], replicated, may hold values from 0.2 to 1
- bin_response: float32 [2048, 8], replicated, may hold values from 0.1 to 1
- observed: float32 [2048, 64], replicated, may hold values from -6 to 6
- obs_var: float32 [2048], replicated, may hold values from 0.1 to 1
- batch_order: int32 [2048], replicated, may hold values from 0 to 2047, each once
Outputs:
- analysis: float32 [64, 8, 32768], P(None, None, ('zrow', 'zcol'))
- obs_analysis: float32 [2, 64, 1024], P(None, None, ('zrow', 'zcol'))
All inputs are finite; a program needn't handle non-finite values.
Results may differ from a plain program's by a relative error of at most 0.0003.
Values sent between devices are 32-bit elements; how exact they have to be, the bound alone decides.
No kernel may reach another device: no remote copies, remote signals or barrier semaphores. Data moves between devices by JAX's collectives and lax.ppermute only.
A program may use at most 128 MiB of HBM per device.

v0:
```python
import jax
import jax.numpy as jnp
from jax import lax
from jax.sharding import PartitionSpec as P

BLK = 128
P_SIZE = 1024
BATCHES = 2


def shards(state, kernel, blocks, foot_weight, bin_response, observed, obs_var, batch_order):
    members = state.shape[0]
    nbins = state.shape[1]
    cells = state.shape[2]
    nblocks = cells // BLK
    devices = lax.axis_size(("zrow", "zcol"))
    myself = lax.axis_index(("zrow", "zcol"))
    share = P_SIZE // devices
    high = lax.Precision.HIGHEST
    center = jnp.eye(members, dtype=jnp.float32) - 1.0 / members
    ident = jnp.eye(members, dtype=jnp.float32)

    def batch_ids(batch):
        return batch_order[batch * P_SIZE : (batch + 1) * P_SIZE]

    def observe(means, batch):
        chosen = batch_ids(batch)
        local_blocks = blocks[chosen] - myself * nblocks
        onehot = (
            local_blocks[:, :, None] == jnp.arange(nblocks, dtype=jnp.int32)[None, None, :]
        ).astype(jnp.float32)
        spread = jnp.sum(onehot * foot_weight[chosen][:, :, None], axis=1)
        weights = (bin_response[chosen][:, :, None] * spread[:, None, :]).reshape(
            P_SIZE, nbins * nblocks
        )
        return lax.dot_general(
            means.reshape(members, nbins * nblocks),
            weights,
            (((1,), (1,)), ((), ())),
            precision=high,
        )

    block_weighted = state.reshape(members, nbins, nblocks, BLK) * kernel.reshape(nblocks, BLK)
    means = jnp.sum(block_weighted, axis=3) / BLK
    priors = lax.psum_scatter(
        jnp.stack([observe(means, batch) for batch in range(BATCHES)]),
        ("zrow", "zcol"),
        scatter_dimension=2,
        tiled=True,
    )
    total = ident
    self_sums = []
    obs_sums = []
    for batch in range(BATCHES):
        mine = lax.dynamic_slice_in_dim(batch_ids(batch), myself * share, share, 0)
        weighted = priors[batch] / obs_var[mine][None, :]
        self_sums.append(jnp.dot(weighted, priors[batch].T, precision=high))
        obs_sums.append(jnp.dot(weighted, observed[mine], precision=high))
    self_all, obs_all = lax.psum((jnp.stack(self_sums), jnp.stack(obs_sums)), ("zrow", "zcol"))
    for batch in range(BATCHES):
        left = jnp.dot(center, total, precision=high)
        inner = jnp.dot(jnp.dot(left, self_all[batch], precision=high), left.T, precision=high)
        residue = obs_all[batch] - jnp.dot(self_all[batch], total.T, precision=high)
        cross = jnp.dot(left, residue, precision=high)
        factor = jnp.linalg.cholesky((members - 1) * ident + inner)
        gain = jax.scipy.linalg.cho_solve((factor, True), cross)
        total = jnp.dot(ident + jnp.dot(gain.T, center, precision=high), total, precision=high)
    field = jnp.dot(total, state.reshape(members, -1), precision=high).reshape(
        members, nbins, cells
    )
    finals = jnp.einsum("ij,tjp->tip", total, priors, precision=high)
    return (field, finals)


def solution(mesh):
    return jax.shard_map(
        shards,
        mesh=mesh,
        in_specs=(
            P(None, None, ("zrow", "zcol")),
            P(("zrow", "zcol")),
            P(),
            P(),
            P(),
            P(),
            P(),
            P(),
        ),
        out_specs=(P(None, None, ("zrow", "zcol")), P(None, None, ("zrow", "zcol"))),
        check_vma=False,
    )
```

profile of v0, /device:TPU:0, one launch (start us, length us, event | category | flops | bytes accessed | tf_op | source)
XLA Modules:
  0.0 347.9 jit_solution(2390267959956065888)
XLA Ops:
  7.9 1.1 copy.94
  9.1 4.0 %gather_fusion.4 = s32[1024,4]{1,0:T(8,128)} fusion(s32[2048,4]{1,0:T(8,128)S(1)} %copy.94, s32[1024]{0:T(1024)S(1)} %get-tuple-element.24), kind=kCustom, calls=%fused_computation.4 | custom fusion | bytes 36864 | tf_op jit(solution)/shard_map/gather | solution.py:28
  13.1 4.0 %gather_fusion.1 = s32[1024,4]{1,0:T(8,128)} fusion(s32[2048,4]{1,0:T(8,128)S(1)} %copy.94, s32[1024]{0:T(1024)S(1)} %get-tuple-element.23), kind=kCustom, calls=%fused_computation.1 | custom fusion | bytes 36864 | tf_op jit(solution)/shard_map/gather | solution.py:28
  17.4 4.0 %gather_fusion.5 = f32[1024,4]{1,0:T(8,128)} fusion(f32[2048,4]{1,0:T(8,128)S(1)} %copy.96, s32[1024]{0:T(1024)S(1)} %get-tuple-element.24), kind=kCustom, calls=%fused_computation.5 | custom fusion | bytes 36864 | tf_op jit(solution)/shard_map/gather | solution.py:32
  21.5 4.0 %gather_fusion.2 = f32[1024,4]{1,0:T(8,128)} fusion(f32[2048,4]{1,0:T(8,128)S(1)} %copy.96, s32[1024]{0:T(1024)S(1)} %get-tuple-element.23), kind=kCustom, calls=%fused_computation.2 | custom fusion | bytes 36864 | tf_op jit(solution)/shard_map/gather | solution.py:32
  25.8 4.0 %gather_fusion.3 = f32[1024,8]{1,0:T(8,128)} fusion(f32[2048,8]{1,0:T(8,128)S(1)} %copy.92, s32[1024]{0:T(1024)S(1)} %get-tuple-element.24), kind=kCustom, calls=%fused_computation.3 | custom fusion | bytes 69632 | tf_op jit(solution)/shard_map/gather | solution.py:33
  29.8 4.0 %gather_fusion = f32[1024,8]{1,0:T(8,128)} fusion(f32[2048,8]{1,0:T(8,128)S(1)} %copy.92, s32[1024]{0:T(1024)S(1)} %get-tuple-element.23), kind=kCustom, calls=%fused_computation | custom fusion | bytes 69632 | tf_op jit(solution)/shard_map/gather | solution.py:33
  34.5 1.2 copy.95
  36.0 1.2 copy.97
  37.4 1.2 copy.93
  38.6 1.2 copy.99
  40.8 1.3 copy.104
  43.9 1.4 copy.107
  46.6 128.3 %all-reduce.5.cloned.1.call-done = f32[2,64,1024]{1,0,2:T(2,128)} async-done(((f32[2,64,1024]{1,0,2:T(2,128)}), f32[2,64,1024]{1,0,2:T(2,128)}) %all-reduce.5.cloned.1.call-update) | async-done | bytes 524304
  174.9 1.0 broadcast_divide_fusion.1
  179.0 124.9 %all-reduce.7.cloned.1.call-done = (f32[2,64,64]{2,1,0:T(8,128)}, f32[2,64,64]{2,1,0:T(8,128)}) async-done(((f32[2,64,64]{2,1,0:T(8,128)}, f32[2,64,64]{2,1,0:T(8,128)}), (f32[2,64,64]{2,1,0:T(8,128)}, f32[2,64,64]{2,1,0:T(8,128)})) %all-reduce.7.cloned.1.call-update) | async-done | bytes 65552 | tf_op jit(solution)/shard_map/psum | solution.py:59
  304.9 0.9 fusion.28
  306.2 5.8 %cholesky.44 = f32[64,64]{1,0:T(8,128)S(1)} custom-call(f32[64,64]{1,0:T(8,128)S(1)} %fusion.23), custom_call_target="Cholesky" | custom-call | tf_op jit(solution)/shard_map/jit(cholesky)/cholesky | solution.py:65
  313.4 4.9 %custom-call.8 = f32[1,64,64]{1,2,0:T(8,128)S(1)} custom-call(f32[1,64,64]{2,1,0:T(8,128)S(1)} %fusion.12), custom_call_target="InvertDiagBlocksLowerTriangular" | custom-call | tf_op jit(solution)/shard_map/jit(_cho_solve)/triangular_solve | solution.py:66
  319.1 1.0 convolution_subtract_fusion
  321.7 5.8 %cholesky.55 = f32[64,64]{1,0:T(8,128)S(1)} custom-call(f32[64,64]{1,0:T(8,128)S(1)} %fusion.18), custom_call_target="Cholesky" | custom-call | tf_op jit(solution)/shard_map/jit(cholesky)/cholesky | solution.py:65
  328.9 4.9 %custom-call.9 = f32[1,64,64]{1,2,0:T(8,128)S(1)} custom-call(f32[1,64,64]{2,1,0:T(8,128)S(1)} %fusion.13), custom_call_target="InvertDiagBlocksLowerTriangular" | custom-call | tf_op jit(solution)/shard_map/jit(_cho_solve)/triangular_solve | solution.py:66
  335.5 3.0 fusion
  338.5 2.5 copy.115
  (72 shorter events, 17.8 us)
Async XLA Ops:
  7.2 35.3 %copy-start = (f32[2048]{0:T(1024)S(1)}, f32[2048]{0:T(1024)}, u32[]{:S(2)}) copy-start(f32[2048]{0:T(1024)} %param.17) | copy-start | bytes 24580
  7.2 167.7 %all-reduce.5.cloned.1.call-start = ((), (), s32[]{:S(2)}) async-start(), calls=%async_computation | async-start | bytes 2097152
  13.1 4.0 %copy-start.5 = (f32[2048,4]{0,1:T(4,128)S(1)}, f32[2048,4]{0,1:T(4,128)}, u32[]{:S(2)}) copy-start(f32[2048,4]{0,1:T(4,128)} %param.14) | copy-start | bytes 98308
  21.5 4.0 %copy-start.4 = (f32[2048,8]{0,1:T(8,128)S(1)}, f32[2048,8]{0,1:T(8,128)}, u32[]{:S(2)}) copy-start(f32[2048,8]{0,1:T(8,128)} %param.15) | copy-start | bytes 196612
  29.8 4.0 %copy-start.1 = (f32[64,8,1024]{2,1,0:T(8,128)S(1)}, f32[64,8,1024]{2,1,0:T(8,128)}, u32[]{:S(2)}) copy-start(f32[64,8,1024]{2,1,0:T(8,128)} %param.11) | copy-start | bytes 6291460
  29.8 4.0 %copy-start.6 = (f32[1024]{0:T(1024)S(1)}, f32[1024]{0:T(1024)}, u32[]{:S(2)}) copy-start(f32[1024]{0:T(1024)} %param.12) | copy-start | bytes 12292
  33.8 2.0 copy-start.2
  33.8 3.4 copy-start.3
  42.1 261.8 %all-reduce.7.cloned.1.call-start = ((), (), s32[]{:S(2)}) async-start(), calls=%async_computation.1 | async-start | bytes 262144 | tf_op jit(solution)/shard_map/psum | solution.py:59
Sparse Core Ops, SparseCore 0:
  42.2 132.5 all-reduce.4
  182.1 121.7 all-reduce.6
where the time goes:
time: 349 us; the launch traced here: 348 us
  waiting for transfers between devices  253 us (72%)
  local copies, waits for them, and re-layouts  39.9 us (11%)
  other arithmetic  27.9 us (8%)
  between operations  14.4 us (4%)
  matrix products  12.2 us (3%)
    unnamed x3, waiting for transfers between devices  128 us
    psum x1, waiting for transfers between devices, shards(): lax.psum((jnp.stack(self_sums), jnp.stack(obs_sums)), ('zrow', 'zcol'))  125 us
    another operation x6, other arithmetic, shards(): factor = jnp.linalg.cholesky((members - 1) * ident + inner)  13 us
    another operation x4, other arithmetic, shards(): gain = jax.scipy.linalg.cho_solve((factor, True), cross)  11.1 us
    gather x4, local copies, waits for them, and re-layouts, observe(): bin_response[chosen][:, :, None] * spread[:, None, :]  10.4 us
    gather x4, local copies, waits for them, and re-layouts, observe(): spread = jnp.sum(onehot * foot_weight[chosen][:, :, None], axis=1)  9.45 us
    gather x4, local copies, waits for them, and re-layouts, observe(): local_blocks = blocks[chosen] - myself * nblocks  9.42 us
  transfers between devices with their start and end apart: 2, of which 2 were waited for; matrix products, arithmetic and copies ran while one was open for 1% of the time, Pallas kernels for 0%

commit v1 on v0

--- a/solution.py
+++ b/solution.py
@@ -56,7 +56,9 @@
         weighted = priors[batch] / obs_var[mine][None, :]
         self_sums.append(jnp.dot(weighted, priors[batch].T, precision=high))
         obs_sums.append(jnp.dot(weighted, observed[mine], precision=high))
-    self_all, obs_all = lax.psum((jnp.stack(self_sums), jnp.stack(obs_sums)), ("zrow", "zcol"))
+    self_all, obs_all = lax.psum(
+        lax.psum((jnp.stack(self_sums), jnp.stack(obs_sums)), "zcol"), "zrow"
+    )
     for batch in range(BATCHES):
         left = jnp.dot(center, total, precision=high)
         inner = jnp.dot(jnp.dot(left, self_all[batch], precision=high), left.T, precision=high)

time: 349 us -> 312 us (0.89)
  waiting for transfers between devices: 253 us -> 216 us
    psum x1 -> x2, waiting for transfers between devices: 125 us -> 87.6 us  [the longest x1 52.2 us: shards(): lax.psum((jnp.stack(self_sums), jnp.stack(obs_sums)), 'zcol')]
    unnamed x3 -> x4, waiting for transfers between devices: 128 us -> 129 us
  transfers between devices with their start and end apart: 2 -> 3, of which waited for: 2 -> 3; matrix products, arithmetic and copies ran while one was open for 1% -> 2% of each run, Pallas kernels for 0% -> 0%
where the time goes in v1:
time: 312 us; the launch traced here: 311 us
  waiting for transfers between devices  216 us (69%)
  local copies, waits for them, and re-layouts  39.9 us (13%)
  other arithmetic  27.9 us (9%)
  between operations  14.1 us (5%)
  matrix products  12.2 us (4%)
    unnamed x4, waiting for transfers between devices  129 us
    psum x1, waiting for transfers between devices, shards(): lax.psum((jnp.stack(self_sums), jnp.stack(obs_sums)), 'zcol')  52.2 us
    psum x1, waiting for transfers between devices, shards(): lax.psum(lax.psum((jnp.stack(self_sums), jnp.stack(obs_sums)), 'zcol'), '...  35.5 us
    another operation x6, other arithmetic, shards(): factor = jnp.linalg.cholesky((members - 1) * ident + inner)  13 us
    another operation x4, other arithmetic, shards(): gain = jax.scipy.linalg.cho_solve((factor, True), cross)  11.1 us
    gather x4, local copies, waits for them, and re-layouts, observe(): bin_response[chosen][:, :, None] * spread[:, None, :]  10.4 us
    gather x4, local copies, waits for them, and re-layouts, observe(): spread = jnp.sum(onehot * foot_weight[chosen][:, :, None], axis=1)  9.45 us
    gather x4, local copies, waits for them, and re-layouts, observe(): local_blocks = blocks[chosen] - myself * nblocks  9.42 us
  transfers between devices with their start and end apart: 3, of which 3 were waited for; matrix products, arithmetic and copies ran while one was open for 2% of the time, Pallas kernels for 0%

profile of v1, /device:TPU:0, one launch (start us, length us, event | category | flops | bytes accessed | tf_op | source)
XLA Modules:
  0.0 310.8 jit_solution(9592850189965675017)
XLA Ops:
  7.9 1.1 copy.94
  9.1 4.0 %gather_fusion.4 = s32[1024,4]{1,0:T(8,128)} fusion(s32[2048,4]{1,0:T(8,128)S(1)} %copy.94, s32[1024]{0:T(1024)S(1)} %get-tuple-element.26), kind=kCustom, calls=%fused_computation.4 | custom fusion | bytes 36864 | tf_op jit(solution)/shard_map/gather | solution.py:28
  13.1 4.0 %gather_fusion.1 = s32[1024,4]{1,0:T(8,128)} fusion(s32[2048,4]{1,0:T(8,128)S(1)} %copy.94, s32[1024]{0:T(1024)S(1)} %get-tuple-element.25), kind=kCustom, calls=%fused_computation.1 | custom fusion | bytes 36864 | tf_op jit(solution)/shard_map/gather | solution.py:28
  17.4 4.0 %gather_fusion.5 = f32[1024,4]{1,0:T(8,128)} fusion(f32[2048,4]{1,0:T(8,128)S(1)} %copy.96, s32[1024]{0:T(1024)S(1)} %get-tuple-element.26), kind=kCustom, calls=%fused_computation.5 | custom fusion | bytes 36864 | tf_op jit(solution)/shard_map/gather | solution.py:32
  21.5 4.0 %gather_fusion.2 = f32[1024,4]{1,0:T(8,128)} fusion(f32[2048,4]{1,0:T(8,128)S(1)} %copy.96, s32[1024]{0:T(1024)S(1)} %get-tuple-element.25), kind=kCustom, calls=%fused_computation.2 | custom fusion | bytes 36864 | tf_op jit(solution)/shard_map/gather | solution.py:32
  25.8 4.0 %gather_fusion.3 = f32[1024,8]{1,0:T(8,128)} fusion(f32[2048,8]{1,0:T(8,128)S(1)} %copy.92, s32[1024]{0:T(1024)S(1)} %get-tuple-element.26), kind=kCustom, calls=%fused_computation.3 | custom fusion | bytes 69632 | tf_op jit(solution)/shard_map/gather | solution.py:33
  29.8 4.0 %gather_fusion = f32[1024,8]{1,0:T(8,128)} fusion(f32[2048,8]{1,0:T(8,128)S(1)} %copy.92, s32[1024]{0:T(1024)S(1)} %get-tuple-element.25), kind=kCustom, calls=%fused_computation | custom fusion | bytes 69632 | tf_op jit(solution)/shard_map/gather | solution.py:33
  34.5 1.2 copy.95
  36.0 1.2 copy.97
  37.4 1.2 copy.93
  38.6 1.2 copy.99
  40.8 1.3 copy.104
  43.7 1.4 copy.107
  46.2 128.7 %all-reduce.7.cloned.1.call-done = f32[2,64,1024]{1,0,2:T(2,128)} async-done(((f32[2,64,1024]{1,0,2:T(2,128)}), f32[2,64,1024]{1,0,2:T(2,128)}) %all-reduce.7.cloned.1.call-update) | async-done | bytes 524304
  174.9 1.0 broadcast_divide_fusion.1
  178.7 52.2 %all-reduce.9.cloned.1.call-done = (f32[2,64,64]{2,1,0:T(8,128)}, f32[2,64,64]{2,1,0:T(8,128)}) async-done(((f32[2,64,64]{2,1,0:T(8,128)}, f32[2,64,64]{2,1,0:T(8,128)}), (f32[2,64,64]{2,1,0:T(8,128)}, f32[2,64,64]{2,1,0:T(8,128)})) %all-reduce.9.cloned.1.call-update) | async-done | bytes 65552 | tf_op jit(solution)/shard_map/psum | solution.py:60
  231.7 35.5 %all-reduce.11.cloned.1.call-done = (f32[2,64,64]{2,1,0:T(8,128)}, f32[2,64,64]{2,1,0:T(8,128)}) async-done(((f32[2,64,64]{2,1,0:T(8,128)}, f32[2,64,64]{2,1,0:T(8,128)}), (f32[2,64,64]{2,1,0:T(8,128)}, f32[2,64,64]{2,1,0:T(8,128)})) %all-reduce.11.cloned.1.call-update) | async-done | bytes 65552 | tf_op jit(solution)/shard_map/psum | solution.py:59
  269.5 5.8 %cholesky.44 = f32[64,64]{1,0:T(8,128)S(1)} custom-call(f32[64,64]{1,0:T(8,128)S(1)} %fusion.23), custom_call_target="Cholesky" | custom-call | tf_op jit(solution)/shard_map/jit(cholesky)/cholesky | solution.py:67
  276.6 4.9 %custom-call.8 = f32[1,64,64]{1,2,0:T(8,128)S(1)} custom-call(f32[1,64,64]{2,1,0:T(8,128)S(1)} %fusion.12), custom_call_target="InvertDiagBlocksLowerTriangular" | custom-call | tf_op jit(solution)/shard_map/jit(_cho_solve)/triangular_solve | solution.py:68
  282.4 1.0 convolution_subtract_fusion
  285.0 5.8 %cholesky.55 = f32[64,64]{1,0:T(8,128)S(1)} custom-call(f32[64,64]{1,0:T(8,128)S(1)} %fusion.18), custom_call_target="Cholesky" | custom-call | tf_op jit(solution)/shard_map/jit(cholesky)/cholesky | solution.py:67
  292.1 4.9 %custom-call.9 = f32[1,64,64]{1,2,0:T(8,128)S(1)} custom-call(f32[1,64,64]{2,1,0:T(8,128)S(1)} %fusion.13), custom_call_target="InvertDiagBlocksLowerTriangular" | custom-call | tf_op jit(solution)/shard_map/jit(_cho_solve)/triangular_solve | solution.py:68
  298.7 3.0 fusion
  301.7 2.5 copy.115
  (75 shorter events, 18.7 us)
Async XLA Ops:
  7.2 35.1 %copy-start = (f32[2048]{0:T(1024)S(1)}, f32[2048]{0:T(1024)}, u32[]{:S(2)}) copy-start(f32[2048]{0:T(1024)} %param.17) | copy-start | bytes 24580
  7.2 167.7 %all-reduce.7.cloned.1.call-start = ((), (), s32[]{:S(2)}) async-start(), calls=%async_computation | async-start | bytes 2097152
  13.1 4.0 %copy-start.5 = (f32[2048,4]{0,1:T(4,128)S(1)}, f32[2048,4]{0,1:T(4,128)}, u32[]{:S(2)}) copy-start(f32[2048,4]{0,1:T(4,128)} %param.14) | copy-start | bytes 98308
  21.5 4.0 %copy-start.4 = (f32[2048,8]{0,1:T(8,128)S(1)}, f32[2048,8]{0,1:T(8,128)}, u32[]{:S(2)}) copy-start(f32[2048,8]{0,1:T(8,128)} %param.15) | copy-start | bytes 196612
  29.8 4.0 %copy-start.1 = (f32[64,8,1024]{2,1,0:T(8,128)S(1)}, f32[64,8,1024]{2,1,0:T(8,128)}, u32[]{:S(2)}) copy-start(f32[64,8,1024]{2,1,0:T(8,128)} %param.11) | copy-start | bytes 6291460
  29.8 4.0 %copy-start.6 = (f32[1024]{0:T(1024)S(1)}, f32[1024]{0:T(1024)}, u32[]{:S(2)}) copy-start(f32[1024]{0:T(1024)} %param.12) | copy-start | bytes 12292
  33.8 2.0 copy-start.2
  33.8 3.4 %copy-start.3 = (f32[1024,4]{1,0:T(8,128)S(1)}, f32[1024,4]{1,0:T(8,128)}, u32[]{:S(2)}) copy-start(f32[1024,4]{1,0:T(8,128)} %gather_fusion.5) | copy-start | bytes 49156
  42.1 188.7 %all-reduce.9.cloned.1.call-start = ((), (), s32[]{:S(2)}) async-start(), calls=%async_computation.1 | async-start | bytes 262144 | tf_op jit(solution)/shard_map/psum | solution.py:60
  178.3 88.9 %all-reduce.11.cloned.1.call-start = ((), (), s32[]{:S(2)}) async-start(), calls=%async_computation.2 | async-start | bytes 262144 | tf_op jit(solution)/shard_map/psum | solution.py:59
Sparse Core Ops, SparseCore 0:
  42.2 132.5 all-reduce.6
  178.8 51.9 all-reduce.8
  233.2 33.8 all-reduce.10
